TPU v7x, 512 devices: a whole 4x4x16 slice. The times are simulated.
512 devices in a mesh: replica: 32 (over z, core), tensor: 16 (over x, y).
Axes of the slice: x: 4, y: 4, z: 16, core: 2. Of those that a mesh axis runs over, the one named last changes fastest.
Arguments:
- x_input: bfloat16 [8192, 4096], P('replica', 'tensor'), may hold values from -6 to 6
- z_input: bfloat16 [8192, 4096], P('replica', 'tensor'), may hold values from -6 to 6
- bc_input: bfloat16 [8192, 1024], P('replica'), may hold values from -6 to 6
- dt_raw: float32 [8192, 128], P('replica', 'tensor'), may hold values from -6 to 6
- dt_bias: float32 [128], P('tensor'), may hold values from -3 to -1
- decay_rates: float32 [128], P('tensor'), may hold values from 0.005 to 0.5
- skip_gain: float32 [128], P('tensor'), may hold values from 0.5 to 1.5
- conv_x: float32 [4, 4096], P(None, 'tensor'), may hold values from -3 to 3
- conv_bc: float32 [4, 1024], replicated, may hold values from -3 to 3
- norm_gain: float32 [4096], P('tensor'), may hold values from 0.5 to 1.5
- out_weight: bfloat16 [4096, 4096], P('tensor'), may hold values from -0.09375 to 0.09375
- cached_states: float32 [64, 128, 32, 128], P('replica', 'tensor'), may hold values from -4 to 4
- cached_tail_x: float32 [64, 3, 4096], P('replica', None, 'tensor'), may hold values from -6 to 6
- cached_tail_bc: float32 [64, 3, 1024], P('replica'), may hold values from -6 to 6
- prefix_block: int32 [64], replicated, may hold values from 0 to 63, as said below
- lengths: int32 [64], P('replica'), may hold values from 128 to 128, as said below
Outputs:
- mixed: bfloat16 [8192, 4096], P(('replica', 'tensor'))
- final_states: float32 [64, 128, 32, 128], P('replica', 'tensor')
Inputs may be any that keep to these rules, and one draw needn't show every extreme that they name: A permutation: request q (on replica q // 2) starts from cached block prefix_block[q], which replica prefix_block[q] // 2 holds; every cached block feeds exactly one request. `lengths`: every request's suffix fills all 128 of its slots, so every entry is 128.
All inputs are finite; a program needn't handle non-finite values.
Results may differ from a plain program's by a relative error of at most 0.015.
Values may be sent and summed in bfloat16 or wider, within the bound.
A program may use at most 64 MiB of HBM per device.

v0:
```python
import jax
import jax.numpy as jnp
from jax import lax
from jax.sharding import PartitionSpec as P

HEADS = 128
HEAD_DIM = 32
STATE = 128
GROUPS = 4
highest = lax.Precision.HIGHEST
epsilon = 1e-05


def causal_conv(tail_rows, sequence, kernel):
    joined = jnp.concatenate([tail_rows, sequence], axis=0)
    length = sequence.shape[0]
    total = joined[0:length] * kernel[0][None, :]
    for offset in range(1, kernel.shape[0]):
        total = total + joined[offset : offset + length] * kernel[offset][None, :]
    return jax.nn.silu(total)


def span_scan(inputs, b_heads, c_heads, step_sizes, decay_rates, skip_gain, carry_state):
    logdec = -step_sizes * decay_rates[None, :]
    cumulative = jnp.cumsum(logdec, axis=0)
    count_rows = inputs.shape[0]
    causal = jnp.arange(count_rows)[:, None] >= jnp.arange(count_rows)[None, :]
    cum_heads = jnp.transpose(cumulative)
    differ = cum_heads[:, :, None] - cum_heads[:, None, :]
    decays = jnp.where(causal[None, :, :], jnp.exp(jnp.minimum(differ, 0.0)), 0.0)
    scores = jnp.einsum("ihn,jhn->hij", c_heads, b_heads, precision=highest)
    weights = scores * decays * jnp.transpose(step_sizes)[:, None, :]
    inside = jnp.einsum("hij,jhp->ihp", weights, inputs, precision=highest)
    carried = jnp.exp(cumulative)[:, :, None] * jnp.einsum(
        "ihn,hpn->ihp", c_heads, carry_state, precision=highest
    )
    output = inside + carried + skip_gain[None, :, None] * inputs
    ending = cumulative[-1]
    weigh_in = jnp.exp(ending[None, :] - cumulative) * step_sizes
    new_state = jnp.exp(ending)[:, None, None] * carry_state + jnp.einsum(
        "jh,jhp,jhn->hpn", weigh_in, inputs, b_heads, precision=highest
    )
    return (output, new_state)


def local(
    x_input,
    z_input,
    bc_input,
    dt_raw,
    dt_bias,
    decay_rates,
    skip_gain,
    conv_x,
    conv_bc,
    norm_gain,
    out_weight,
    cached_states,
    cached_tail_x,
    cached_tail_bc,
    prefix_block,
    lengths,
):
    requests = lengths.shape[0]
    local_heads = dt_raw.shape[1]
    tokens_dev = x_input.shape[0]
    slot_len = tokens_dev // requests
    wanted = lax.dynamic_slice_in_dim(prefix_block, lax.axis_index("replica") * requests, requests)
    empty_carry = (
        jnp.zeros_like(cached_states),
        jnp.zeros_like(cached_tail_x),
        jnp.zeros_like(cached_tail_bc),
    )
    pick_pieces = (
        lax.all_gather(cached_states.astype(jnp.bfloat16), "replica", axis=0, tiled=True).astype(
            jnp.float32
        ),
        lax.all_gather(cached_tail_x.astype(jnp.bfloat16), "replica", axis=0, tiled=True).astype(
            jnp.float32
        ),
        lax.all_gather(cached_tail_bc.astype(jnp.bfloat16), "replica", axis=0, tiled=True).astype(
            jnp.float32
        ),
    )
    count_blocks = pick_pieces[0].shape[0]
    inside = (wanted >= 0) & (wanted < count_blocks)
    position = jnp.clip(wanted, 0, count_blocks - 1)
    chosen = []
    for current, piece in zip(empty_carry, pick_pieces):
        taken_rows = jnp.take(piece, position, axis=0)
        in_mask = inside.reshape((requests,) + (1,) * (current.ndim - 1))
        chosen.append(jnp.where(in_mask, taken_rows, current))
    start_states, start_tail_x, start_tail_bc = tuple(chosen)
    head_ids = lax.axis_index("tensor") * local_heads + jnp.arange(local_heads)
    member = ((head_ids // (HEADS // GROUPS))[:, None] == jnp.arange(GROUPS)[None, :]).astype(
        jnp.float32
    )
    live = jnp.arange(slot_len)[None, :] < lengths[:, None]
    outputs = []
    finals = []
    for request in range(requests):
        row_lo = request * slot_len
        row_hi = row_lo + slot_len
        inputs = causal_conv(
            start_tail_x[request], x_input[row_lo:row_hi].astype(jnp.float32), conv_x
        ).reshape(slot_len, local_heads, HEAD_DIM)
        bc_conv = causal_conv(
            start_tail_bc[request], bc_input[row_lo:row_hi].astype(jnp.float32), conv_bc
        )
        b_groups = bc_conv[:, : GROUPS * STATE].reshape(slot_len, GROUPS, STATE)
        c_groups = bc_conv[:, GROUPS * STATE :].reshape(slot_len, GROUPS, STATE)
        b_heads = jnp.einsum("lgn,hg->lhn", b_groups, member, precision=highest)
        c_heads = jnp.einsum("lgn,hg->lhn", c_groups, member, precision=highest)
        step_sizes = jnp.where(
            live[request][:, None], jax.nn.softplus(dt_raw[row_lo:row_hi] + dt_bias[None, :]), 0.0
        )
        carry_state = start_states[request]
        output, carry_state = span_scan(
            inputs, b_heads, c_heads, step_sizes, decay_rates, skip_gain, carry_state
        )
        outputs.append(output.reshape(slot_len, -1))
        finals.append(carry_state)
    outputs = jnp.concatenate(outputs, axis=0)
    final_states = jnp.stack(finals, axis=0)
    gate_vals = outputs * jax.nn.silu(z_input.astype(jnp.float32))
    by_head = gate_vals.reshape(tokens_dev, local_heads, HEAD_DIM)
    head_squares = jnp.sum(by_head * by_head, axis=2)
    partial_sq = jnp.dot(head_squares, member, precision=highest)
    totals = lax.psum(partial_sq, "tensor")
    mean_sq = jnp.dot(totals, jnp.transpose(member), precision=highest) / (
        HEADS * HEAD_DIM // GROUPS
    )
    normed = (by_head * lax.rsqrt(mean_sq + epsilon)[:, :, None]).reshape(
        tokens_dev, -1
    ) * norm_gain[None, :]
    gated = jnp.where(live.reshape(tokens_dev, 1), normed, 0.0).astype(jnp.bfloat16)
    mixed = lax.psum_scatter(
        jnp.dot(gated, out_weight, preferred_element_type=jnp.float32).astype(jnp.bfloat16),
        "tensor",
        scatter_dimension=0,
        tiled=True,
    )
    return (mixed, final_states)


def solution(mesh):
    placed = (
        P("replica", "tensor"),
        P("replica", "tensor"),
        P("replica", None),
        P("replica", "tensor"),
        P("tensor"),
        P("tensor"),
        P("tensor"),
        P(None, "tensor"),
        P(),
        P("tensor"),
        P("tensor", None),
        P("replica", "tensor", None, None),
        P("replica", None, "tensor"),
        P("replica", None, None),
        P(),
        P("replica"),
    )
    return jax.shard_map(
        local,
        mesh=mesh,
        in_specs=placed,
        out_specs=(P(("replica", "tensor"), None), P("replica", "tensor", None, None)),
        check_vma=False,
    )
```

profile of v0, /device:TPU:2, one launch (start us, length us, event | category | flops | bytes accessed | tf_op | source)
XLA Modules:
  0.0 261.4 jit_solution(10844467314238256731)
XLA Ops:
  7.2 1.8 convert_element_type.46
  9.1 1.3 fusion.71
  15.1 37.8 %all_gather.10 = bf16[64,3,1024]{2,1,0:T(4,128)(2,1)S(1)} all-gather(bf16[2,3,1024]{2,1,0:T(4,128)(2,1)S(1)} %copy.87), channel_id=1, replica_groups=mesh['replica'=32,'tensor'=16] {'replica'}, dimensions={0}, use_global_device_ids=true | all-gather | bytes 405504 | tf_op jit(solution)/shard_map/all_gather | solution.py:81
  53.9 1.1 slice_convert_fusion.1
  57.6 27.6 %all_gather.9 = bf16[64,3,256]{2,1,0:T(4,128)(2,1)S(1)} all-gather(bf16[2,3,256]{2,1,0:T(4,128)(2,1)S(1)} %copy.85), channel_id=1, replica_groups=mesh['replica'=32,'tensor'=16] {'replica'}, dimensions={0}, use_global_device_ids=true | all-gather | bytes 101376 | tf_op jit(solution)/shard_map/all_gather | solution.py:78
  85.9 1.6 gather_fusion
  93.1 1.5 copy.93
  95.4 1.5 copy.101
  97.0 1.7 copy.103
  98.7 1.4 exponential_multiply_fusion.1
  100.6 1.4 convolution_bitcast_fusion.3
  102.0 1.3 fusion.1
  103.3 1.6 convolution_bitcast_fusion.7
  104.9 1.4 convolution_bitcast_fusion
  106.7 1.3 fusion
  108.0 1.6 convolution_bitcast_fusion.5
  109.6 6.6 %convert_element_type.47 = f32[64,8,32,128]{3,2,1,0:T(8,128)} convert(bf16[64,8,32,128]{3,2,1,0:T(8,128)(2,1)} %all-gather.2.cloned.1.call-done) | non-fusion elementwise | flops 2097152 | bytes 12582912 | tf_op jit(solution)/shard_map/convert_element_type | solution.py:75
  116.3 4.8 %gather_fusion.2 = f32[2,8,32,128]{3,2,1,0:T(8,128)} fusion(f32[64,8,32,128]{3,2,1,0:T(8,128)} %convert_element_type.47, s32[1024]{0:T(1024)} %copy-done.18), kind=kCustom, calls=%fused_computation.2 | custom fusion | bytes 524296 | tf_op jit(solution)/shard_map/jit(_take)/gather | solution.py:90
  122.1 2.1 fusion.9
  124.2 2.1 fusion.6
  127.2 35.1 %psum.7 = f32[256,4]{0,1:T(4,128)} all-reduce(f32[256,4]{0,1:T(4,128)S(1)} %fusion.65), channel_id=1, replica_groups=mesh['replica'=32,'tensor'=16] {'tensor'}, use_global_device_ids=true, to_apply=%region_3.4 | all-reduce | flops 1024 | bytes 8192 | tf_op jit(solution)/shard_map/psum | solution.py:129
  164.3 2.1 convolution_convert_fusion
  167.8 1.5 fusion.3
  170.6 83.9 %reduce-scatter.2.cloned.1.call-done = bf16[16,4096]{1,0:T(8,128)(2,1)} async-done(((bf16[256,4096]{1,0:T(8,128)(2,1)}), bf16[16,4096]{1,0:T(8,128)(2,1)}) %reduce-scatter.2.cloned.1.call-update) | async-done | bytes 131088 | tf_op jit(solution)/shard_map/reduce_scatter | solution.py:137
  (104 shorter events, 22.9 us)
Async XLA Ops:
  7.2 157.1 %copy-start = (bf16[256,4096]{1,0:T(8,128)(2,1)S(1)}, bf16[256,4096]{1,0:T(8,128)(2,1)}, u32[]{:S(2)}) copy-start(bf16[256,4096]{1,0:T(8,128)(2,1)} %param.26) | copy-start | bytes 6291460
  7.2 45.9 %copy-start.23 = (s32[64]{0:T(128)S(1)}, s32[64]{0:T(128)}, u32[]{:S(2)}) copy-start(s32[64]{0:T(128)} %param.30) | copy-start | bytes 772
  7.2 46.6 %copy-start.12 = (f32[4,1024]{1,0:T(4,128)S(1)}, f32[4,1024]{1,0:T(4,128)}, u32[]{:S(2)}) copy-start(f32[4,1024]{1,0:T(4,128)} %param.24) | copy-start | bytes 49156
  7.2 102.4 %all-gather.2.cloned.1.call-start = ((), (), s32[]{:S(2)}) async-start(), calls=%async_computation.1 | async-start | bytes 4325376 | tf_op jit(solution)/shard_map/all_gather | solution.py:75
  9.0 245.5 %reduce-scatter.2.cloned.1.call-start = ((), (), s32[]{:S(2)}) async-start(), calls=%async_computation.2 | async-start | bytes 2228224 | tf_op jit(solution)/shard_map/reduce_scatter | solution.py:137
  10.4 2.4 copy-start.20
  10.4 2.4 copy-start.21
  11.5 87.2 %copy-start.4 = (f32[128,8]{1,0:T(8,128)}, f32[128,8]{1,0:T(8,128)S(1)}, u32[]{:S(2)}) copy-start(f32[128,8]{1,0:T(8,128)S(1)} %reduce_window_sum.17) | copy-start | bytes 12292
  13.1 85.6 %copy-start.5 = (f32[128,8]{1,0:T(8,128)}, f32[128,8]{1,0:T(8,128)S(1)}, u32[]{:S(2)}) copy-start(f32[128,8]{1,0:T(8,128)S(1)} %reduce_window_sum.18) | copy-start | bytes 12292
  53.2 2.5 copy-start.16
  53.2 34.4 %copy-start.15 = (pred[2]{0:T(512)(128)(4,1)}, pred[2]{0:T(512)(128)(4,1)S(1)}, u32[]{:S(2)}) copy-start(pred[2]{0:T(512)(128)(4,1)S(1)} %get-tuple-element.4) | copy-start | bytes 10
  53.2 2.5 copy-start.18
  55.1 2.5 copy-start.19
  55.7 31.8 %copy-start.22 = (f32[4,256]{1,0:T(4,128)S(1)}, f32[4,256]{1,0:T(4,128)}, u32[]{:S(2)}) copy-start(f32[4,256]{1,0:T(4,128)} %param.23) | copy-start | bytes 12292
  55.8 31.8 %copy-start.17 = (pred[2]{0:T(512)(128)(4,1)S(1)}, pred[2]{0:T(512)(128)(4,1)}, u32[]{:S(2)}) copy-start(pred[2]{0:T(512)(128)(4,1)} %copy-done.16) | copy-start | bytes 10
  57.6 41.1 %copy-start.8 = (f32[256,8]{0,1:T(8,128)S(1)}, f32[256,8]{0,1:T(8,128)}, u32[]{:S(2)}) copy-start(f32[256,8]{0,1:T(8,128)} %param.19) | copy-start | bytes 24580
  90.4 12.8 %copy-start.3 = (f32[128,256]{0,1:T(8,128)}, f32[128,256]{0,1:T(8,128)S(1)}, u32[]{:S(2)}) copy-start(f32[128,256]{0,1:T(8,128)S(1)} %copy.86) | copy-start | bytes 393220
  98.6 7.6 %copy-start.13 = (s32[8]{0:T(128)}, s32[8]{0:T(128)S(1)}, u32[]{:S(2)}) copy-start(s32[8]{0:T(128)S(1)} %and_select_fusion) | copy-start | bytes 100
  100.6 5.7 %copy-start.6 = (f32[128,4,128]{2,1,0:T(4,128)S(1)}, f32[128,4,128]{2,1,0:T(4,128)}, u32[]{:S(2)}) copy-start(f32[128,4,128]{2,1,0:T(4,128)} %reshape.123) | copy-start | bytes 786436
  102.0 6.0 %copy-start.1 = (f32[128,8,128]{2,1,0:T(8,128)}, f32[128,8,128]{2,1,0:T(8,128)S(1)}, u32[]{:S(2)}) copy-start(f32[128,8,128]{2,1,0:T(8,128)S(1)} %convolution_bitcast_fusion.3) | copy-start | bytes 1572868
  109.6 12.5 %copy-start.10 = (f32[128,8]{0,1:T(8,128)S(1)}, f32[128,8]{0,1:T(8,128)}, u32[]{:S(2)}) copy-start(f32[128,8]{0,1:T(8,128)} %copy.93) | copy-start | bytes 12292
  116.3 8.0 %copy-start.11 = (f32[128,8]{0,1:T(8,128)S(1)}, f32[128,8]{0,1:T(8,128)}, u32[]{:S(2)}) copy-start(f32[128,8]{0,1:T(8,128)} %copy.101) | copy-start | bytes 12292
  116.3 10.8 %copy-start.14 = (s32[8]{0:T(128)S(1)}, s32[8]{0:T(128)}, u32[]{:S(2)}) copy-start(s32[8]{0:T(128)} %copy-done.13) | copy-start | bytes 100
  121.0 5.2 %copy-start.7 = (bf16[256,256]{0,1:T(8,128)(2,1)S(1)}, bf16[256,256]{0,1:T(8,128)(2,1)}, u32[]{:S(2)}) copy-start(bf16[256,256]{0,1:T(8,128)(2,1)} %copy.103) | copy-start | bytes 393220
  (2 other events, 2.7 us)
Sparse Core Ops, SparseCore 0:
  10.1 78.4 all-gather.1
  166.5 87.9 reduce-scatter.1
where the time goes:
time: 262 us; the launch traced here: 261 us
  blocking collectives  100 us (38%)
  waiting for transfers between devices  83.9 us (32%)
  local copies, waits for them, and re-layouts  22.3 us (9%)
  other arithmetic  21.4 us (8%)
  matrix products  18.7 us (7%)
  between operations  14.5 us (6%)
    reduce_scatter x1, waiting for transfers between devices, local(): lax.psum_scatter(jnp.dot(gated, out_weight, preferred_element_type=jnp.fl...  83.9 us
    all_gather x1, blocking collectives, local(): lax.all_gather(cached_tail_bc.astype(jnp.bfloat16), 'replica', axis=0, ti...  37.8 us
    psum x1, blocking collectives, local(): totals = lax.psum(partial_sq, 'tensor')  35.1 us
    all_gather x1, blocking collectives, local(): lax.all_gather(cached_tail_x.astype(jnp.bfloat16), 'replica', axis=0, til...  27.6 us
    gather x3, local copies, waits for them, and re-layouts, local(): taken_rows = jnp.take(piece, position, axis=0)  6.99 us
    convert_element_type x1, other arithmetic, local(): lax.all_gather(cached_states.astype(jnp.bfloat16), 'replica', axis=0, til...  6.65 us
  transfers between devices with their start and end apart: 2, of which 1 were waited for; matrix products, arithmetic and copies ran while one was open for 15% of the time, Pallas kernels for 0%

commit v1 on v0

--- a/solution.py
+++ b/solution.py
@@ -126,7 +126,9 @@
     by_head = gate_vals.reshape(tokens_dev, local_heads, HEAD_DIM)
     head_squares = jnp.sum(by_head * by_head, axis=2)
     partial_sq = jnp.dot(head_squares, member, precision=highest)
-    totals = lax.psum(partial_sq, "tensor")
+    totals = partial_sq
+    for hop in (1, 2, 4, 8):
+        totals = totals + lax.ppermute(totals, "tensor", [(dev, dev ^ hop) for dev in range(16)])
     mean_sq = jnp.dot(totals, jnp.transpose(member), precision=highest) / (
         HEADS * HEAD_DIM // GROUPS
     )

time: 262 us -> 249 us (0.950)
  blocking collectives: 100 us -> 65.4 us
  starting transfers between devices: 0.08 us -> 15.1 us
  waiting for transfers between devices: 83.9 us -> 93.3 us
    psum x1 -> x0, blocking collectives: 35.1 us -> none  [local(): totals = lax.psum(partial_sq, 'tensor')]
    ppermute x0 -> x4, starting transfers between devices: none -> 15 us  [local(): lax.ppermute(totals, 'tensor', [(dev, dev ^ hop) for dev in range(16)])]
    ppermute x0 -> x4, waiting for transfers between devices: none -> 9.9 us  [local(): lax.ppermute(totals, 'tensor', [(dev, dev ^ hop) for dev in range(16)])]
  transfers between devices with their start and end apart: 2 -> 6, of which waited for: 1 -> 5; matrix products, arithmetic and copies ran while one was open for 15% -> 16% of each run, Pallas kernels for 0% -> 0%
where the time goes in v1:
time: 249 us; the launch traced here: 248 us
  waiting for transfers between devices  93.3 us (37%)
  blocking collectives  65.4 us (26%)
  local copies, waits for them, and re-layouts  22.3 us (9%)
  other arithmetic  19.7 us (8%)
  matrix products  18 us (7%)
  starting transfers between devices  15.1 us (6%)
  between operations  14.6 us (6%)
    reduce_scatter x1, waiting for transfers between devices, local(): lax.psum_scatter(jnp.dot(gated, out_weight, preferred_element_type=jnp.fl...  83.4 us
    all_gather x1, blocking collectives, local(): lax.all_gather(cached_tail_bc.astype(jnp.bfloat16), 'replica', axis=0, ti...  37.9 us
    all_gather x1, blocking collectives, local(): lax.all_gather(cached_tail_x.astype(jnp.bfloat16), 'replica', axis=0, til...  27.5 us
    ppermute x4, starting transfers between devices, local(): lax.ppermute(totals, 'tensor', [(dev, dev ^ hop) for dev in range(16)])  15 us
    ppermute x4, waiting for transfers between devices, local(): lax.ppermute(totals, 'tensor', [(dev, dev ^ hop) for dev in range(16)])  9.9 us
    gather x3, local copies, waits for them, and re-layouts, local(): taken_rows = jnp.take(piece, position, axis=0)  6.99 us
    convert_element_type x1, other arithmetic, local(): lax.all_gather(cached_states.astype(jnp.bfloat16), 'replica', axis=0, til...  6.66 us
  transfers between devices with their start and end apart: 6, of which 5 were waited for; matrix products, arithmetic and copies ran while one was open for 16% of the time, Pallas kernels for 0%

profile of v1, /device:TPU:2, one launch (start us, length us, event | category | flops | bytes accessed | tf_op | source)
XLA Modules:
  0.0 248.4 jit_solution(1251152126528130021)
XLA Ops:
  7.2 1.8 convert_element_type.46
  15.2 37.9 %all_gather.10 = bf16[64,3,1024]{2,1,0:T(4,128)(2,1)S(1)} all-gather(bf16[2,3,1024]{2,1,0:T(4,128)(2,1)S(1)} %copy.87), channel_id=1, replica_groups=mesh['replica'=32,'tensor'=16] {'replica'}, dimensions={0}, use_global_device_ids=true | all-gather | bytes 405504 | tf_op jit(solution)/shard_map/all_gather | solution.py:81
  57.7 27.5 %all_gather.9 = bf16[64,3,256]{2,1,0:T(4,128)(2,1)S(1)} all-gather(bf16[2,3,256]{2,1,0:T(4,128)(2,1)S(1)} %copy.85), channel_id=1, replica_groups=mesh['replica'=32,'tensor'=16] {'replica'}, dimensions={0}, use_global_device_ids=true | all-gather | bytes 101376 | tf_op jit(solution)/shard_map/all_gather | solution.py:78
  85.9 1.6 gather_fusion
  93.1 1.5 copy.93
  95.4 1.5 copy.101
  97.0 1.7 copy.103
  103.3 1.6 convolution_bitcast_fusion.7
  108.0 1.6 convolution_bitcast_fusion.5
  109.6 6.7 %convert_element_type.47 = f32[64,8,32,128]{3,2,1,0:T(8,128)} convert(bf16[64,8,32,128]{3,2,1,0:T(8,128)(2,1)} %all-gather.2.cloned.1.call-done) | non-fusion elementwise | flops 2097152 | bytes 12582912 | tf_op jit(solution)/shard_map/convert_element_type | solution.py:75
  116.2 4.8 %gather_fusion.2 = f32[2,8,32,128]{3,2,1,0:T(8,128)} fusion(f32[64,8,32,128]{3,2,1,0:T(8,128)} %convert_element_type.47, s32[1024]{0:T(1024)} %copy-done.18), kind=kCustom, calls=%fused_computation.2 | custom fusion | bytes 524296 | tf_op jit(solution)/shard_map/jit(_take)/gather | solution.py:90
  122.1 2.1 fusion.9
  124.2 2.1 fusion.6
  126.5 3.6 %collective-permute-start = (f32[256,4]{0,1:T(4,128)S(1)}, f32[256,4]{0,1:T(4,128)S(1)}, u32[]{:S(2)}, u32[]{:S(2)}) collective-permute-start(f32[256,4]{0,1:T(4,128)S(1)} %fusion.66), channel_id=1, source_target_pairs={{0,1},{1,0},{2,3},{3,2},{4,5},{5,4},{6,7},{7,6},{8,9},{9,8},{10,11... | collective-permute-start | bytes 12296 | tf_op jit(solution)/shard_map/ppermute | solution.py:131
  130.1 1.9 collective-permute-done
  132.0 5.1 %collective-permute-start.1 = (f32[256,4]{0,1:T(4,128)S(1)}, f32[256,4]{0,1:T(4,128)S(1)}, u32[]{:S(2)}, u32[]{:S(2)}) collective-permute-start(f32[256,4]{0,1:T(4,128)S(1)} %add.169), channel_id=1, source_target_pairs={{0,2},{1,3},{2,0},{3,1},{4,6},{5,7},{6,4},{7,5},{8,10},{9,11},{10,... | collective-permute-start | bytes 12296 | tf_op jit(solution)/shard_map/ppermute | solution.py:131
  137.1 1.9 collective-permute-done.1
  139.0 2.4 collective-permute-start.2
  141.4 3.1 %collective-permute-done.2 = f32[256,4]{0,1:T(4,128)S(1)} collective-permute-done((f32[256,4]{0,1:T(4,128)S(1)}, f32[256,4]{0,1:T(4,128)S(1)}, u32[]{:S(2)}, u32[]{:S(2)}) %collective-permute-start.2) | collective-permute-done | bytes 4128 | tf_op jit(solution)/shard_map/ppermute | solution.py:131
  144.5 4.0 %collective-permute-start.3 = (f32[256,4]{0,1:T(4,128)S(1)}, f32[256,4]{0,1:T(4,128)S(1)}, u32[]{:S(2)}, u32[]{:S(2)}) collective-permute-start(f32[256,4]{0,1:T(4,128)S(1)} %add.171), channel_id=1, source_target_pairs={{0,8},{1,9},{2,10},{3,11},{4,12},{5,13},{6,14},{7,15},{8,0},{9,1},... | collective-permute-start | bytes 12296 | tf_op jit(solution)/shard_map/ppermute | solution.py:131
  148.5 3.0 %collective-permute-done.3 = f32[256,4]{0,1:T(4,128)S(1)} collective-permute-done((f32[256,4]{0,1:T(4,128)S(1)}, f32[256,4]{0,1:T(4,128)S(1)}, u32[]{:S(2)}, u32[]{:S(2)}) %collective-permute-start.3) | collective-permute-done | bytes 4128 | tf_op jit(solution)/shard_map/ppermute | solution.py:131
  151.8 2.1 convolution_convert_fusion
  155.3 1.5 fusion.3
  158.2 83.4 %reduce-scatter.2.cloned.1.call-done = bf16[16,4096]{1,0:T(8,128)(2,1)} async-done(((bf16[256,4096]{1,0:T(8,128)(2,1)}), bf16[16,4096]{1,0:T(8,128)(2,1)}) %reduce-scatter.2.cloned.1.call-update) | async-done | bytes 131088 | tf_op jit(solution)/shard_map/reduce_scatter | solution.py:139
  (118 shorter events, 29.7 us)
Async XLA Ops:
  7.2 144.7 %copy-start = (bf16[256,4096]{1,0:T(8,128)(2,1)S(1)}, bf16[256,4096]{1,0:T(8,128)(2,1)}, u32[]{:S(2)}) copy-start(bf16[256,4096]{1,0:T(8,128)(2,1)} %param.26) | copy-start | bytes 6291460
  7.2 46.0 %copy-start.25 = (s32[64]{0:T(128)S(1)}, s32[64]{0:T(128)}, u32[]{:S(2)}) copy-start(s32[64]{0:T(128)} %param.30) | copy-start | bytes 772
  7.2 46.7 %copy-start.12 = (f32[4,1024]{1,0:T(4,128)S(1)}, f32[4,1024]{1,0:T(4,128)}, u32[]{:S(2)}) copy-start(f32[4,1024]{1,0:T(4,128)} %param.24) | copy-start | bytes 49156
  7.2 102.4 %all-gather.2.cloned.1.call-start = ((), (), s32[]{:S(2)}) async-start(), calls=%async_computation.1 | async-start | bytes 4325376 | tf_op jit(solution)/shard_map/all_gather | solution.py:75
  9.0 232.5 %reduce-scatter.2.cloned.1.call-start = ((), (), s32[]{:S(2)}) async-start(), calls=%async_computation.2 | async-start | bytes 2228224 | tf_op jit(solution)/shard_map/reduce_scatter | solution.py:139
  11.5 87.1 %copy-start.4 = (f32[128,8]{1,0:T(8,128)}, f32[128,8]{1,0:T(8,128)S(1)}, u32[]{:S(2)}) copy-start(f32[128,8]{1,0:T(8,128)S(1)} %reduce_window_sum.17) | copy-start | bytes 12292
  13.1 85.6 %copy-start.5 = (f32[128,8]{1,0:T(8,128)}, f32[128,8]{1,0:T(8,128)S(1)}, u32[]{:S(2)}) copy-start(f32[128,8]{1,0:T(8,128)S(1)} %reduce_window_sum.18) | copy-start | bytes 12292
  53.3 34.3 %copy-start.15 = (pred[2]{0:T(512)(128)(4,1)}, pred[2]{0:T(512)(128)(4,1)S(1)}, u32[]{:S(2)}) copy-start(pred[2]{0:T(512)(128)(4,1)S(1)} %get-tuple-element.4) | copy-start | bytes 10
  55.8 31.8 %copy-start.22 = (f32[4,256]{1,0:T(4,128)S(1)}, f32[4,256]{1,0:T(4,128)}, u32[]{:S(2)}) copy-start(f32[4,256]{1,0:T(4,128)} %param.23) | copy-start | bytes 12292
  55.8 31.8 %copy-start.17 = (pred[2]{0:T(512)(128)(4,1)S(1)}, pred[2]{0:T(512)(128)(4,1)}, u32[]{:S(2)}) copy-start(pred[2]{0:T(512)(128)(4,1)} %copy-done.16) | copy-start | bytes 10
  57.7 41.0 %copy-start.8 = (f32[256,8]{0,1:T(8,128)S(1)}, f32[256,8]{0,1:T(8,128)}, u32[]{:S(2)}) copy-start(f32[256,8]{0,1:T(8,128)} %param.19) | copy-start | bytes 24580
  90.4 12.8 %copy-start.3 = (f32[128,256]{0,1:T(8,128)}, f32[128,256]{0,1:T(8,128)S(1)}, u32[]{:S(2)}) copy-start(f32[128,256]{0,1:T(8,128)S(1)} %copy.86) | copy-start | bytes 393220
  98.6 7.6 %copy-start.13 = (s32[8]{0:T(128)}, s32[8]{0:T(128)S(1)}, u32[]{:S(2)}) copy-start(s32[8]{0:T(128)S(1)} %and_select_fusion) | copy-start | bytes 100
  100.5 5.7 %copy-start.6 = (f32[128,4,128]{2,1,0:T(4,128)S(1)}, f32[128,4,128]{2,1,0:T(4,128)}, u32[]{:S(2)}) copy-start(f32[128,4,128]{2,1,0:T(4,128)} %reshape.123) | copy-start | bytes 786436
  102.0 6.0 %copy-start.1 = (f32[128,8,128]{2,1,0:T(8,128)}, f32[128,8,128]{2,1,0:T(8,128)S(1)}, u32[]{:S(2)}) copy-start(f32[128,8,128]{2,1,0:T(8,128)S(1)} %convolution_bitcast_fusion.3) | copy-start | bytes 1572868
  109.6 12.5 %copy-start.10 = (f32[128,8]{0,1:T(8,128)S(1)}, f32[128,8]{0,1:T(8,128)}, u32[]{:S(2)}) copy-start(f32[128,8]{0,1:T(8,128)} %copy.93) | copy-start | bytes 12292
  116.2 8.0 %copy-start.11 = (f32[128,8]{0,1:T(8,128)S(1)}, f32[128,8]{0,1:T(8,128)}, u32[]{:S(2)}) copy-start(f32[128,8]{0,1:T(8,128)} %copy.101) | copy-start | bytes 12292
  116.2 10.1 %copy-start.14 = (s32[8]{0:T(128)S(1)}, s32[8]{0:T(128)}, u32[]{:S(2)}) copy-start(s32[8]{0:T(128)} %copy-done.13) | copy-start | bytes 100
  121.0 30.7 %copy-start.23 = (f32[256]{0:T(256)S(1)}, f32[256]{0:T(256)}, u32[]{:S(2)}) copy-start(f32[256]{0:T(256)} %param.25) | copy-start | bytes 3076
  121.0 30.7 %copy-start.24 = (pred[256]{0:T(512)(128)(4,1)S(1)}, pred[256]{0:T(512)(128)(4,1)}, u32[]{:S(2)}) copy-start(pred[256]{0:T(512)(128)(4,1)} %get-tuple-element.38) | copy-start | bytes 772
  126.5 5.5 %collective-permute-start = (f32[256,4]{0,1:T(4,128)S(1)}, f32[256,4]{0,1:T(4,128)S(1)}, u32[]{:S(2)}, u32[]{:S(2)}) collective-permute-start(f32[256,4]{0,1:T(4,128)S(1)} %fusion.66), channel_id=1, source_target_pairs={{0,1},{1,0},{2,3},{3,2},{4,5},{5,4},{6,7},{7,6},{8,9},{9,8},{10,11... | collective-permute-start | bytes 12296 | tf_op jit(solution)/shard_map/ppermute | solution.py:131
  132.0 7.0 %collective-permute-start.1 = (f32[256,4]{0,1:T(4,128)S(1)}, f32[256,4]{0,1:T(4,128)S(1)}, u32[]{:S(2)}, u32[]{:S(2)}) collective-permute-start(f32[256,4]{0,1:T(4,128)S(1)} %add.169), channel_id=1, source_target_pairs={{0,2},{1,3},{2,0},{3,1},{4,6},{5,7},{6,4},{7,5},{8,10},{9,11},{10,... | collective-permute-start | bytes 12296 | tf_op jit(solution)/shard_map/ppermute | solution.py:131
  139.0 5.5 %collective-permute-start.2 = (f32[256,4]{0,1:T(4,128)S(1)}, f32[256,4]{0,1:T(4,128)S(1)}, u32[]{:S(2)}, u32[]{:S(2)}) collective-permute-start(f32[256,4]{0,1:T(4,128)S(1)} %add.170), channel_id=1, source_target_pairs={{0,4},{1,5},{2,6},{3,7},{4,0},{5,1},{6,2},{7,3},{8,12},{9,13},{10,... | collective-permute-start | bytes 12296 | tf_op jit(solution)/shard_map/ppermute | solution.py:131
  144.5 7.0 %collective-permute-start.3 = (f32[256,4]{0,1:T(4,128)S(1)}, f32[256,4]{0,1:T(4,128)S(1)}, u32[]{:S(2)}, u32[]{:S(2)}) collective-permute-start(f32[256,4]{0,1:T(4,128)S(1)} %add.171), channel_id=1, source_target_pairs={{0,8},{1,9},{2,10},{3,11},{4,12},{5,13},{6,14},{7,15},{8,0},{9,1},... | collective-permute-start | bytes 12296 | tf_op jit(solution)/shard_map/ppermute | solution.py:131
  (8 other events, 20.4 us)
Sparse Core Ops, SparseCore 0:
  10.1 78.5 all-gather.1
  154.1 87.4 reduce-scatter.1
